TPU v7x, 128 devices: a whole 4x4x4 slice. The times are simulated.
128 devices in a mesh: dp: 8 (over z, core), mp: 16 (over x, y).
Axes of the slice: x: 4, y: 4, z: 4, core: 2. Of those that a mesh axis runs over, the one named last changes fastest.
Arguments:
- activations: bfloat16 [16384, 5120], P(('dp', 'mp')), may hold values from -10 to 10
- cotangent: bfloat16 [16384, 5120], P('dp', 'mp'), may hold values from -1 to 1
- master_weights: float32 [5120, 5120], P('dp', 'mp'), may hold values from -32 to 32
- first_moment: float32 [5120, 5120], P('dp', 'mp'), may hold values from -1 to 1
- second_moment: float32 [5120, 5120], P('dp', 'mp'), may hold values from 0.25 to 4
- step_count: int32 [1], replicated, may hold values from 1 to 23
- language_ids: int32 [1], replicated, may hold values from 0 to 7
- language_rates: float32 [8], replicated, may hold values from 0.25 to 2
Outputs:
- new_master: float32 [5120, 5120], P('dp', 'mp')
- new_first: float32 [5120, 5120], P('dp', 'mp')
- new_second: float32 [5120, 5120], P('dp', 'mp')
- new_weights: bfloat16 [5120, 5120], P(None, 'mp')
All inputs are finite; a program needn't handle non-finite values.
Results may differ from a plain program's by a relative error of at most 0.0004.
Values may be sent and summed in bfloat16 or wider, within the bound.
No kernel may reach another device: no remote copies, remote signals or barrier semaphores. Data moves between devices by JAX's collectives and lax.ppermute only.
A program may use at most 128 MiB of HBM per device.

v0:
```python
import jax
import jax.numpy as jnp
from jax import lax
from jax.sharding import PartitionSpec as P

beta_one = 0.9
beta_two = 0.999
epsilon = 1e-06
decay_weight = 0.1
base_rate = 0.25


def on_device(
    activations,
    cotangent,
    master_weights,
    first_moment,
    second_moment,
    step_count,
    language_ids,
    language_rates,
):
    gathered = lax.all_gather(activations, "mp", axis=0, tiled=True)
    gradient = lax.psum_scatter(
        lax.dot_general(
            gathered, cotangent, (((0,), (0,)), ((), ())), preferred_element_type=jnp.float32
        ),
        "dp",
        scatter_dimension=0,
        tiled=True,
    )
    steps_done = step_count[0].astype(jnp.float32)
    corr_one = 1.0 - jnp.power(jnp.float32(beta_one), steps_done)
    corr_two = 1.0 - jnp.power(jnp.float32(beta_two), steps_done)
    new_first = beta_one * first_moment + (1.0 - beta_one) * gradient
    new_second = beta_two * second_moment + (1.0 - beta_two) * gradient * gradient
    update = (
        new_first / corr_one / (jnp.sqrt(new_second / corr_two) + epsilon)
        + decay_weight * master_weights
    )
    weight_sq, update_sq = lax.psum(
        (jnp.sum(master_weights * master_weights), jnp.sum(update * update)), ("dp", "mp")
    )
    trust = jnp.sqrt(weight_sq) / jnp.sqrt(update_sq)
    picked = jnp.arange(language_rates.shape[0], dtype=jnp.int32) == language_ids[0]
    rate = base_rate * jnp.sum(jnp.where(picked, language_rates, jnp.float32(0.0)))
    new_master = master_weights - rate * trust * update
    new_weights = lax.all_gather(new_master.astype(jnp.bfloat16), "dp", axis=0, tiled=True)
    return (new_master, new_first, new_second, new_weights)


def solution(mesh):
    return jax.shard_map(
        on_device,
        mesh=mesh,
        in_specs=(
            P(("dp", "mp"), None),
            P("dp", "mp"),
            P("dp", "mp"),
            P("dp", "mp"),
            P("dp", "mp"),
            P(),
            P(),
            P(),
        ),
        out_specs=(P("dp", "mp"), P("dp", "mp"), P("dp", "mp"), P(None, "mp")),
        check_vma=False,
    )
```

profile of v0, /device:TPU:1, one launch (start us, length us, event | category | flops | bytes accessed | tf_op | source)
XLA Modules:
  0.0 311.8 jit_solution(5477487466860797035)
XLA Ops:
  7.2 0.0 copy-start
  7.2 0.0 all-gather.3.cloned.1.call-start
  7.2 0.7 all-gather.3.cloned.1.call-update
  7.9 0.0 reduce-scatter.2.cloned.1.call-start
  8.0 138.1 %all-gather.3.cloned.1.call-done = bf16[2048,5120]{1,0:T(8,128)(2,1)} async-done(((bf16[128,5120]{1,0:T(8,128)(2,1)}), bf16[2048,5120]{1,0:T(8,128)(2,1)}) %all-gather.3.cloned.1.call-update) | async-done | bytes 20971536 | tf_op jit(solution)/shard_map/all_gather | solution.py:23
  146.0 0.0 copy-done
  146.0 13.9 %fusion.4 = f32[5120,320]{0,1:T(8,128)} fusion(bf16[2048,320]{0,1:T(8,128)(2,1)S(1)} %copy-done, bf16[2048,5120]{1,0:T(8,128)(2,1)} %all-gather.3.cloned.1.call-done), kind=kOutput, calls=%fused_computation.10 | convolution fusion | flops 6710886400 | bytes 28835840 | tf_op jit(solution)/shard_map/dot_general | solution.py:25
  159.9 0.0 copy-start.2
  159.9 0.0 copy-start.1
  159.9 0.0 reduce-scatter.2.cloned.1.call-update
  160.0 0.0 all-gather.5.cloned.1.call-start
  161.5 0.0 copy-done.2
  161.5 0.6 fusion.1
  162.7 40.4 %reduce-scatter.2.cloned.1.call-done = f32[640,320]{0,1:T(8,128)} async-done(((f32[5120,320]{0,1:T(8,128)}), f32[640,320]{0,1:T(8,128)}) %reduce-scatter.2.cloned.1.call-update) | async-done | bytes 819216 | tf_op jit(solution)/shard_map/reduce_scatter | solution.py:24
  203.1 0.0 copy-done.1
  203.1 4.1 %multiply_reduce_fusion = (f32[]{:T(128)}, f32[640,320]{0,1:T(8,128)S(1)}, f32[640,320]{0,1:T(8,128)}, f32[640,320]{0,1:T(8,128)}, f32[]{:T(128)}) fusion(f32[640,320]{0,1:T(8,128)S(1)} %copy-done.1, f32[]{:T(128)} %bitcast.2, f32[]{:T(128)} %bitcast.1, f32[640,320]{0,1:T(8,128)} %reduce-scatter.2.cloned.1.call-done, f32[640,320]{0,1:T(8,128)} %param.12, ...), kind=kLoop, calls=%fused_computation.3 | loop fusion | flops 3481598 | bytes 5734416 | tf_op jit(solution)/shard_map/reduce_sum | solution.py:42
  207.2 66.1 %all-reduce = (f32[]{:T(128)}, f32[]{:T(128)}) all-reduce(f32[]{:T(128)} %get-tuple-element.12, f32[]{:T(128)} %get-tuple-element.8), channel_id=1, replica_groups=mesh['dp'=8,'mp'=16] {'dp','mp'}, use_global_device_ids=true, to_apply=%region_2.0 | all-reduce | flops 2 | bytes 16 | tf_op jit(solution)/shard_map/psum | solution.py:41
  274.7 1.1 fusion.2
  275.8 0.0 all-gather.5.cloned.1.call-update
  275.8 25.6 %all-gather.5.cloned.1.call-done = bf16[5120,320]{0,1:T(8,128)(2,1)} async-done(((bf16[640,320]{0,1:T(8,128)(2,1)}), bf16[5120,320]{0,1:T(8,128)(2,1)}) %all-gather.5.cloned.1.call-update) | async-done | bytes 3276816 | tf_op jit(solution)/shard_map/all_gather | solution.py:48
  301.4 3.8 %copy.15 = bf16[5120,320]{0,1:T(8,128)(2,1)} copy(bf16[5120,320]{0,1:T(8,128)(2,1)} %all-gather.5.cloned.1.call-done) | data formatting | bytes 6553600
Async XLA Ops:
  7.2 138.9 %copy-start = (bf16[2048,320]{0,1:T(8,128)(2,1)S(1)}, bf16[2048,320]{0,1:T(8,128)(2,1)}, u32[]{:S(2)}) copy-start(bf16[2048,320]{0,1:T(8,128)(2,1)} %param.9) | copy-start | bytes 3932164
  7.2 138.9 %all-gather.3.cloned.1.call-start = ((), (), s32[]{:S(2)}) async-start(), calls=%async_computation.1 | async-start | bytes 22282240 | tf_op jit(solution)/shard_map/all_gather | solution.py:23
  7.9 195.2 %reduce-scatter.2.cloned.1.call-start = ((), (), s32[]{:S(2)}) async-start(), calls=%async_computation.2 | async-start | bytes 7372800 | tf_op jit(solution)/shard_map/reduce_scatter | solution.py:24
  159.9 1.5 copy-start.2
  159.9 43.2 %copy-start.1 = (f32[640,320]{0,1:T(8,128)S(1)}, f32[640,320]{0,1:T(8,128)}, u32[]{:S(2)}) copy-start(f32[640,320]{0,1:T(8,128)} %param.10) | copy-start | bytes 2457604
  160.0 141.4 %all-gather.5.cloned.1.call-start = ((), (), s32[]{:S(2)}) async-start(), calls=%async_computation.3 | async-start | bytes 3686400 | tf_op jit(solution)/shard_map/all_gather | solution.py:48
Sparse Core Ops, SparseCore 0:
  10.2 135.8 all-gather.2
  160.1 42.9 reduce-scatter.1
  276.0 25.3 all-gather.4
where the time goes:
time: 312 us
  waiting for transfers between devices  205 us (66%)
  blocking collectives  66.1 us (21%)
  between operations  17.2 us (6%)
  matrix products  13.9 us (4%)
  other arithmetic  5.83 us (2%)
  local copies, waits for them, and re-layouts  3.86 us (1%)
    all_gather x1, waiting for transfers between devices, on_device(): gathered = lax.all_gather(activations, 'mp', axis=0, tiled=True)  138 us
    psum x1, blocking collectives, on_device(): lax.psum((jnp.sum(master_weights * master_weights), jnp.sum(update * upda...  66.1 us
    reduce_scatter x1, waiting for transfers between devices, on_device(): lax.psum_scatter(lax.dot_general(gathered, cotangent, (((0,), (0,)), ((),...  40.4 us
    all_gather x1, waiting for transfers between devices, on_device(): lax.all_gather(new_master.astype(jnp.bfloat16), 'dp', axis=0, tiled=True)  25.6 us
    dot_general x1, matrix products, on_device(): lax.dot_general(gathered, cotangent, (((0,), (0,)), ((), ())), preferred_...  13.9 us
  transfers between devices with their start and end apart: 3, of which 3 were waited for; matrix products, arithmetic and copies ran while one was open for 0% of the time, Pallas kernels for 0%

commit v1 on v0

--- a/solution.py
+++ b/solution.py
@@ -20,7 +20,22 @@
     language_ids,
     language_rates,
 ):
-    gathered = lax.all_gather(activations, "mp", axis=0, tiled=True)
+    ways, here, step = (lax.axis_size("mp"), lax.axis_index("mp"), activations.shape[0])
+    shape = [n * ways if d == 0 else n for d, n in enumerate(activations.shape)]
+    gathered = lax.dynamic_update_slice_in_dim(
+        jnp.zeros(shape, activations.dtype), activations, here * step, axis=0
+    )
+    going_up = going_down = activations
+    for far in range(1, ways // 2 + 1):
+        going_up = lax.ppermute(going_up, "mp", [(d, (d + 1) % ways) for d in range(ways)])
+        gathered = lax.dynamic_update_slice_in_dim(
+            gathered, going_up, (here - far) % ways * step, axis=0
+        )
+        if 2 * far < ways:
+            going_down = lax.ppermute(going_down, "mp", [(d, (d - 1) % ways) for d in range(ways)])
+            gathered = lax.dynamic_update_slice_in_dim(
+                gathered, going_down, (here + far) % ways * step, axis=0
+            )
     gradient = lax.psum_scatter(
         lax.dot_general(
             gathered, cotangent, (((0,), (0,)), ((), ())), preferred_element_type=jnp.float32

time: 312 us -> 422 us (1.35)
  starting transfers between devices: 0.12 us -> 37.5 us
  local copies, waits for them, and re-layouts: 3.86 us -> 40.1 us
  waiting for transfers between devices: 205 us -> 240 us
    ppermute x0 -> x15, waiting for transfers between devices: none -> 170 us  [the longest x8 147 us: on_device(): lax.ppermute(going_up, 'mp', [(d, (d + 1) % ways) for d in range(ways)])]
    all_gather x1 -> x0, waiting for transfers between devices: 138 us -> none  [on_device(): gathered = lax.all_gather(activations, 'mp', axis=0, tiled=True)]
    ppermute x0 -> x15, starting transfers between devices: none -> 37.4 us  [the longest x7 35.2 us: on_device(): lax.ppermute(going_down, 'mp', [(d, (d - 1) % ways) for d in range(ways)])]
    dynamic_update_slice x0 -> x16, local copies, waits for them, and re-layouts: none -> 27.8 us  [the longest x8 14.5 us: on_device(): lax.dynamic_update_slice_in_dim(gathered, going_up, (here - far) % ways *...]
    broadcast_in_dim x0 -> x1, local copies, waits for them, and re-layouts: none -> 7.36 us  [on_device(): jnp.zeros(shape, activations.dtype)]
  transfers between devices with their start and end apart: 3 -> 17, of which waited for: 3 -> 14; matrix products, arithmetic and copies ran while one was open for 0% -> 8% of each run, Pallas kernels for 0% -> 0%
where the time goes in v1:
time: 422 us; the launch traced here: 421 us
  waiting for transfers between devices  240 us (57%)
  blocking collectives  66.1 us (16%)
  local copies, waits for them, and re-layouts  40.1 us (10%)
  starting transfers between devices  37.5 us (9%)
  between operations  17.5 us (4%)
  matrix products  14 us (3%)
  other arithmetic  5.83 us (1%)
    ppermute x8, waiting for transfers between devices, on_device(): lax.ppermute(going_up, 'mp', [(d, (d + 1) % ways) for d in range(ways)])  147 us
    psum x1, blocking collectives, on_device(): lax.psum((jnp.sum(master_weights * master_weights), jnp.sum(update * upda...  66.1 us
    reduce_scatter x1, waiting for transfers between devices, on_device(): lax.psum_scatter(lax.dot_general(gathered, cotangent, (((0,), (0,)), ((),...  44.4 us
    ppermute x7, starting transfers between devices, on_device(): lax.ppermute(going_down, 'mp', [(d, (d - 1) % ways) for d in range(ways)])  35.2 us
    all_gather x1, waiting for transfers between devices, on_device(): lax.all_gather(new_master.astype(jnp.bfloat16), 'dp', axis=0, tiled=True)  25.6 us
    ppermute x7, waiting for transfers between devices, on_device(): lax.ppermute(going_down, 'mp', [(d, (d - 1) % ways) for d in range(ways)])  22.7 us
    dynamic_update_slice x8, local copies, waits for them, and re-layouts, on_device(): lax.dynamic_update_slice_in_dim(gathered, going_up, (here - far) % ways *...  14.5 us
    dot_general x1, matrix products, on_device(): lax.dot_general(gathered, cotangent, (((0,), (0,)), ((), ())), preferred_...  14 us
  transfers between devices with their start and end apart: 17, of which 14 were waited for; matrix products, arithmetic and copies ran while one was open for 8% of the time, Pallas kernels for 0%

profile of v1, /device:TPU:1, one launch (start us, length us, event | category | flops | bytes accessed | tf_op | source)
XLA Modules:
  0.0 421.2 jit_solution(16422306052630820339)
XLA Ops:
  7.2 0.0 reduce-scatter.2.cloned.1.call-start
  7.2 2.2 collective-permute-start
  9.4 3.7 collective-permute-start.1
  13.1 28.6 %collective-permute-done = bf16[128,5120]{1,0:T(8,128)(2,1)S(1)} collective-permute-done((bf16[128,5120]{1,0:T(8,128)(2,1)}, bf16[128,5120]{1,0:T(8,128)(2,1)S(1)}, u32[]{:S(2)}, u32[]{:S(2)}) %collective-permute-start) | collective-permute-done | bytes 1310752 | tf_op jit(solution)/shard_map/ppermute | solution.py:30
  41.7 1.1 copy-done.3
  42.8 4.7 %collective-permute-start.3 = (bf16[128,5120]{1,0:T(8,128)(2,1)S(1)}, bf16[128,5120]{1,0:T(8,128)(2,1)}, u32[]{:S(2)}, u32[]{:S(2)}) collective-permute-start(bf16[128,5120]{1,0:T(8,128)(2,1)S(1)} %collective-permute-done.1), channel_id=1, source_target_pairs={{0,15},{1,0},{2,1},{3,2},{4,3},{5,4},{6,5},{7,6},{8,7},{9,8},{10,9... | collective-permute-start | bytes 3932168 | tf_op jit(solution)/shard_map/ppermute | solution.py:35
  47.6 26.6 %collective-permute-done.2 = bf16[128,5120]{1,0:T(8,128)(2,1)} collective-permute-done((bf16[128,5120]{1,0:T(8,128)(2,1)S(1)}, bf16[128,5120]{1,0:T(8,128)(2,1)}, u32[]{:S(2)}, u32[]{:S(2)}) %collective-permute-start.2) | collective-permute-done | bytes 1310752 | tf_op jit(solution)/shard_map/ppermute | solution.py:30
  74.1 5.6 %collective-permute-start.5 = (bf16[128,5120]{1,0:T(8,128)(2,1)}, bf16[128,5120]{1,0:T(8,128)(2,1)}, u32[]{:S(2)}, u32[]{:S(2)}) collective-permute-start(bf16[128,5120]{1,0:T(8,128)(2,1)} %collective-permute-done.3), channel_id=1, source_target_pairs={{0,15},{1,0},{2,1},{3,2},{4,3},{5,4},{6,5},{7,6},{8,7},{9,8},{10,9... | collective-permute-start | bytes 3932168 | tf_op jit(solution)/shard_map/ppermute | solution.py:35
  79.7 26.1 %collective-permute-done.4 = bf16[128,5120]{1,0:T(8,128)(2,1)} collective-permute-done((bf16[128,5120]{1,0:T(8,128)(2,1)}, bf16[128,5120]{1,0:T(8,128)(2,1)}, u32[]{:S(2)}, u32[]{:S(2)}) %collective-permute-start.4) | collective-permute-done | bytes 1310752 | tf_op jit(solution)/shard_map/ppermute | solution.py:30
  105.8 7.4 %broadcast_in_dim.8 = bf16[2048,5120]{1,0:T(8,128)(2,1)} broadcast(bf16[]{:T(256)} %constant.106.clone.1), dimensions={} | broadcast | bytes 20971522 | tf_op jit(solution)/shard_map/broadcast_in_dim | solution.py:26
  113.2 1.2 constant_dynamic-update-slice_fusion.15
  114.4 2.5 constant_dynamic-update-slice_fusion.14
  116.8 4.8 %collective-permute-start.7 = (bf16[128,5120]{1,0:T(8,128)(2,1)}, bf16[128,5120]{1,0:T(8,128)(2,1)S(1)}, u32[]{:S(2)}, u32[]{:S(2)}) collective-permute-start(bf16[128,5120]{1,0:T(8,128)(2,1)} %collective-permute-done.5), channel_id=1, source_target_pairs={{0,15},{1,0},{2,1},{3,2},{4,3},{5,4},{6,5},{7,6},{8,7},{9,8},{10,9... | collective-permute-start | bytes 3932168 | tf_op jit(solution)/shard_map/ppermute | solution.py:35
  121.6 2.5 constant_dynamic-update-slice_fusion.13
  124.1 12.5 %collective-permute-done.6 = bf16[128,5120]{1,0:T(8,128)(2,1)} collective-permute-done((bf16[128,5120]{1,0:T(8,128)(2,1)}, bf16[128,5120]{1,0:T(8,128)(2,1)}, u32[]{:S(2)}, u32[]{:S(2)}) %collective-permute-start.6) | collective-permute-done | bytes 1310752 | tf_op jit(solution)/shard_map/ppermute | solution.py:30
  136.6 2.5 constant_dynamic-update-slice_fusion.12
  139.1 2.5 constant_dynamic-update-slice_fusion.11
  141.5 5.1 %collective-permute-done.7 = bf16[128,5120]{1,0:T(8,128)(2,1)S(1)} collective-permute-done((bf16[128,5120]{1,0:T(8,128)(2,1)}, bf16[128,5120]{1,0:T(8,128)(2,1)S(1)}, u32[]{:S(2)}, u32[]{:S(2)}) %collective-permute-start.7) | collective-permute-done | bytes 1310752 | tf_op jit(solution)/shard_map/ppermute | solution.py:35
  146.6 5.4 %collective-permute-start.9 = (bf16[128,5120]{1,0:T(8,128)(2,1)S(1)}, bf16[128,5120]{1,0:T(8,128)(2,1)S(1)}, u32[]{:S(2)}, u32[]{:S(2)}) collective-permute-start(bf16[128,5120]{1,0:T(8,128)(2,1)S(1)} %collective-permute-done.7), channel_id=1, source_target_pairs={{0,15},{1,0},{2,1},{3,2},{4,3},{5,4},{6,5},{7,6},{8,7},{9,8},{10,9... | collective-permute-start | bytes 3932168 | tf_op jit(solution)/shard_map/ppermute | solution.py:35
  152.0 2.5 constant_dynamic-update-slice_fusion.10
  154.5 11.9 %collective-permute-done.8 = bf16[128,5120]{1,0:T(8,128)(2,1)S(1)} collective-permute-done((bf16[128,5120]{1,0:T(8,128)(2,1)}, bf16[128,5120]{1,0:T(8,128)(2,1)S(1)}, u32[]{:S(2)}, u32[]{:S(2)}) %collective-permute-start.8) | collective-permute-done | bytes 1310752 | tf_op jit(solution)/shard_map/ppermute | solution.py:30
  166.4 2.5 constant_dynamic-update-slice_fusion.9
  168.8 2.5 constant_dynamic-update-slice_fusion.8
  171.3 4.5 %collective-permute-done.9 = bf16[128,5120]{1,0:T(8,128)(2,1)S(1)} collective-permute-done((bf16[128,5120]{1,0:T(8,128)(2,1)S(1)}, bf16[128,5120]{1,0:T(8,128)(2,1)S(1)}, u32[]{:S(2)}, u32[]{:S(2)}) %collective-permute-start.9) | collective-permute-done | bytes 1310752 | tf_op jit(solution)/shard_map/ppermute | solution.py:35
  175.8 5.5 %collective-permute-start.11 = (bf16[128,5120]{1,0:T(8,128)(2,1)S(1)}, bf16[128,5120]{1,0:T(8,128)(2,1)S(1)}, u32[]{:S(2)}, u32[]{:S(2)}) collective-permute-start(bf16[128,5120]{1,0:T(8,128)(2,1)S(1)} %collective-permute-done.9), channel_id=1, source_target_pairs={{0,15},{1,0},{2,1},{3,2},{4,3},{5,4},{6,5},{7,6},{8,7},{9,8},{10,9... | collective-permute-start | bytes 3932168 | tf_op jit(solution)/shard_map/ppermute | solution.py:35
  181.3 1.2 constant_dynamic-update-slice_fusion.7
  182.5 12.5 %collective-permute-done.10 = bf16[128,5120]{1,0:T(8,128)(2,1)S(1)} collective-permute-done((bf16[128,5120]{1,0:T(8,128)(2,1)S(1)}, bf16[128,5120]{1,0:T(8,128)(2,1)S(1)}, u32[]{:S(2)}, u32[]{:S(2)}) %collective-permute-start.10) | collective-permute-done | bytes 1310752 | tf_op jit(solution)/shard_map/ppermute | solution.py:30
  195.0 1.2 constant_dynamic-update-slice_fusion.6
  196.1 1.1 constant_dynamic-update-slice_fusion.5
  197.3 6.8 %collective-permute-done.11 = bf16[128,5120]{1,0:T(8,128)(2,1)S(1)} collective-permute-done((bf16[128,5120]{1,0:T(8,128)(2,1)S(1)}, bf16[128,5120]{1,0:T(8,128)(2,1)S(1)}, u32[]{:S(2)}, u32[]{:S(2)}) %collective-permute-start.11) | collective-permute-done | bytes 1310752 | tf_op jit(solution)/shard_map/ppermute | solution.py:35
  204.1 5.5 %collective-permute-start.13 = (bf16[128,5120]{1,0:T(8,128)(2,1)S(1)}, bf16[128,5120]{1,0:T(8,128)(2,1)S(1)}, u32[]{:S(2)}, u32[]{:S(2)}) collective-permute-start(bf16[128,5120]{1,0:T(8,128)(2,1)S(1)} %collective-permute-done.11), channel_id=1, source_target_pairs={{0,15},{1,0},{2,1},{3,2},{4,3},{5,4},{6,5},{7,6},{8,7},{9,8},{10,9... | collective-permute-start | bytes 3932168 | tf_op jit(solution)/shard_map/ppermute | solution.py:35
  209.6 1.1 constant_dynamic-update-slice_fusion.4
  210.8 11.9 %collective-permute-done.12 = bf16[128,5120]{1,0:T(8,128)(2,1)S(1)} collective-permute-done((bf16[128,5120]{1,0:T(8,128)(2,1)S(1)}, bf16[128,5120]{1,0:T(8,128)(2,1)S(1)}, u32[]{:S(2)}, u32[]{:S(2)}) %collective-permute-start.12) | collective-permute-done | bytes 1310752 | tf_op jit(solution)/shard_map/ppermute | solution.py:30
  222.7 1.2 constant_dynamic-update-slice_fusion.3
  223.9 1.2 constant_dynamic-update-slice_fusion.2
  225.1 6.4 %collective-permute-done.13 = bf16[128,5120]{1,0:T(8,128)(2,1)S(1)} collective-permute-done((bf16[128,5120]{1,0:T(8,128)(2,1)S(1)}, bf16[128,5120]{1,0:T(8,128)(2,1)S(1)}, u32[]{:S(2)}, u32[]{:S(2)}) %collective-permute-start.13) | collective-permute-done | bytes 1310752 | tf_op jit(solution)/shard_map/ppermute | solution.py:35
  231.5 1.1 constant_dynamic-update-slice_fusion.1
  232.7 17.3 %collective-permute-done.14 = bf16[128,5120]{1,0:T(8,128)(2,1)S(1)} collective-permute-done((bf16[128,5120]{1,0:T(8,128)(2,1)S(1)}, bf16[128,5120]{1,0:T(8,128)(2,1)S(1)}, u32[]{:S(2)}, u32[]{:S(2)}) %collective-permute-start.14) | collective-permute-done | bytes 1310752 | tf_op jit(solution)/shard_map/ppermute | solution.py:30
  249.9 1.1 constant_dynamic-update-slice_fusion
  251.1 14.0 %fusion.4 = f32[5120,320]{0,1:T(8,128)} fusion(bf16[2048,320]{0,1:T(8,128)(2,1)S(1)} %copy-done, bf16[2048,5120]{1,0:T(8,128)(2,1)} %constant_dynamic-update-slice_fusion), kind=kOutput, calls=%fused_computation.26 | convolution fusion | flops 6710886400 | bytes 28835840 | tf_op jit(solution)/shard_map/dot_general | solution.py:40
  265.1 0.0 all-gather.2.cloned.1.call-start
  266.5 0.6 fusion.1
  267.8 44.4 %reduce-scatter.2.cloned.1.call-done = f32[640,320]{0,1:T(8,128)} async-done(((f32[5120,320]{0,1:T(8,128)}), f32[640,320]{0,1:T(8,128)}) %reduce-scatter.2.cloned.1.call-update) | async-done | bytes 819216 | tf_op jit(solution)/shard_map/reduce_scatter | solution.py:39
  312.2 4.1 multiply_reduce_fusion
  316.3 66.1 %all-reduce = (f32[]{:T(128)}, f32[]{:T(128)}) all-reduce(f32[]{:T(128)} %get-tuple-element.12, f32[]{:T(128)} %get-tuple-element.8), channel_id=1, replica_groups=mesh['dp'=8,'mp'=16] {'dp','mp'}, use_global_device_ids=true, to_apply=%region_2.3 | all-reduce | flops 2 | bytes 16 | tf_op jit(solution)/shard_map/psum | solution.py:56
  383.7 1.1 fusion.2
  384.9 25.6 %all-gather.2.cloned.1.call-done = bf16[5120,320]{0,1:T(8,128)(2,1)} async-done(((bf16[640,320]{0,1:T(8,128)(2,1)}), bf16[5120,320]{0,1:T(8,128)(2,1)}) %all-gather.2.cloned.1.call-update) | async-done | bytes 3276816 | tf_op jit(solution)/shard_map/all_gather | solution.py:63
  410.5 3.8 copy.31
  (23 shorter events, 0.1 us)
Async XLA Ops:
  7.2 243.9 %copy-start = (bf16[2048,320]{0,1:T(8,128)(2,1)S(1)}, bf16[2048,320]{0,1:T(8,128)(2,1)}, u32[]{:S(2)}) copy-start(bf16[2048,320]{0,1:T(8,128)(2,1)} %param.9) | copy-start | bytes 3932164
  7.2 106.0 %copy-start.2 = (bf16[128,5120]{1,0:T(8,128)(2,1)S(1)}, bf16[128,5120]{1,0:T(8,128)(2,1)}, u32[]{:S(2)}) copy-start(bf16[128,5120]{1,0:T(8,128)(2,1)} %param.8) | copy-start | bytes 3932164
  7.2 305.0 %reduce-scatter.2.cloned.1.call-start = ((), (), s32[]{:S(2)}) async-start(), calls=%async_computation.1 | async-start | bytes 7372800 | tf_op jit(solution)/shard_map/reduce_scatter | solution.py:39
  7.2 34.5 %collective-permute-start = (bf16[128,5120]{1,0:T(8,128)(2,1)}, bf16[128,5120]{1,0:T(8,128)(2,1)S(1)}, u32[]{:S(2)}, u32[]{:S(2)}) collective-permute-start(bf16[128,5120]{1,0:T(8,128)(2,1)} %param.8), channel_id=1, source_target_pairs={{0,1},{1,2},{2,3},{3,4},{4,5},{5,6},{6,7},{7,8},{8,9},{9,10},{10,1... | collective-permute-start | bytes 3932168 | tf_op jit(solution)/shard_map/ppermute | solution.py:30
  9.4 32.3 %collective-permute-start.1 = (bf16[128,5120]{1,0:T(8,128)(2,1)}, bf16[128,5120]{1,0:T(8,128)(2,1)S(1)}, u32[]{:S(2)}, u32[]{:S(2)}) collective-permute-start(bf16[128,5120]{1,0:T(8,128)(2,1)} %param.8), channel_id=1, source_target_pairs={{0,15},{1,0},{2,1},{3,2},{4,3},{5,4},{6,5},{7,6},{8,7},{9,8},{10,9... | collective-permute-start | bytes 3932168 | tf_op jit(solution)/shard_map/ppermute | solution.py:35
  41.7 32.4 %copy-start.4 = (bf16[128,5120]{1,0:T(8,128)(2,1)}, bf16[128,5120]{1,0:T(8,128)(2,1)S(1)}, u32[]{:S(2)}) copy-start(bf16[128,5120]{1,0:T(8,128)(2,1)S(1)} %collective-permute-done) | copy-start | bytes 3932164
  41.7 32.4 %collective-permute-start.2 = (bf16[128,5120]{1,0:T(8,128)(2,1)S(1)}, bf16[128,5120]{1,0:T(8,128)(2,1)}, u32[]{:S(2)}, u32[]{:S(2)}) collective-permute-start(bf16[128,5120]{1,0:T(8,128)(2,1)S(1)} %collective-permute-done), channel_id=1, source_target_pairs={{0,1},{1,2},{2,3},{3,4},{4,5},{5,6},{6,7},{7,8},{8,9},{9,10},{10,1... | collective-permute-start | bytes 3932168 | tf_op jit(solution)/shard_map/ppermute | solution.py:30
  41.7 1.1 copy-start.3
  42.8 31.3 %collective-permute-start.3 = (bf16[128,5120]{1,0:T(8,128)(2,1)S(1)}, bf16[128,5120]{1,0:T(8,128)(2,1)}, u32[]{:S(2)}, u32[]{:S(2)}) collective-permute-start(bf16[128,5120]{1,0:T(8,128)(2,1)S(1)} %collective-permute-done.1), channel_id=1, source_target_pairs={{0,15},{1,0},{2,1},{3,2},{4,3},{5,4},{6,5},{7,6},{8,7},{9,8},{10,9... | collective-permute-start | bytes 3932168 | tf_op jit(solution)/shard_map/ppermute | solution.py:35
  74.1 31.7 %collective-permute-start.4 = (bf16[128,5120]{1,0:T(8,128)(2,1)}, bf16[128,5120]{1,0:T(8,128)(2,1)}, u32[]{:S(2)}, u32[]{:S(2)}) collective-permute-start(bf16[128,5120]{1,0:T(8,128)(2,1)} %collective-permute-done.2), channel_id=1, source_target_pairs={{0,1},{1,2},{2,3},{3,4},{4,5},{5,6},{6,7},{7,8},{8,9},{9,10},{10,1... | collective-permute-start | bytes 3932168 | tf_op jit(solution)/shard_map/ppermute | solution.py:30
  74.1 42.7 %collective-permute-start.5 = (bf16[128,5120]{1,0:T(8,128)(2,1)}, bf16[128,5120]{1,0:T(8,128)(2,1)}, u32[]{:S(2)}, u32[]{:S(2)}) collective-permute-start(bf16[128,5120]{1,0:T(8,128)(2,1)} %collective-permute-done.3), channel_id=1, source_target_pairs={{0,15},{1,0},{2,1},{3,2},{4,3},{5,4},{6,5},{7,6},{8,7},{9,8},{10,9... | collective-permute-start | bytes 3932168 | tf_op jit(solution)/shard_map/ppermute | solution.py:35
  105.8 30.8 %collective-permute-start.6 = (bf16[128,5120]{1,0:T(8,128)(2,1)}, bf16[128,5120]{1,0:T(8,128)(2,1)}, u32[]{:S(2)}, u32[]{:S(2)}) collective-permute-start(bf16[128,5120]{1,0:T(8,128)(2,1)} %collective-permute-done.4), channel_id=1, source_target_pairs={{0,1},{1,2},{2,3},{3,4},{4,5},{5,6},{6,7},{7,8},{8,9},{9,10},{10,1... | collective-permute-start | bytes 3932168 | tf_op jit(solution)/shard_map/ppermute | solution.py:30
  116.8 29.8 %collective-permute-start.7 = (bf16[128,5120]{1,0:T(8,128)(2,1)}, bf16[128,5120]{1,0:T(8,128)(2,1)S(1)}, u32[]{:S(2)}, u32[]{:S(2)}) collective-permute-start(bf16[128,5120]{1,0:T(8,128)(2,1)} %collective-permute-done.5), channel_id=1, source_target_pairs={{0,15},{1,0},{2,1},{3,2},{4,3},{5,4},{6,5},{7,6},{8,7},{9,8},{10,9... | collective-permute-start | bytes 3932168 | tf_op jit(solution)/shard_map/ppermute | solution.py:35
  136.6 29.8 %collective-permute-start.8 = (bf16[128,5120]{1,0:T(8,128)(2,1)}, bf16[128,5120]{1,0:T(8,128)(2,1)S(1)}, u32[]{:S(2)}, u32[]{:S(2)}) collective-permute-start(bf16[128,5120]{1,0:T(8,128)(2,1)} %collective-permute-done.6), channel_id=1, source_target_pairs={{0,1},{1,2},{2,3},{3,4},{4,5},{5,6},{6,7},{7,8},{8,9},{9,10},{10,1... | collective-permute-start | bytes 3932168 | tf_op jit(solution)/shard_map/ppermute | solution.py:30
  146.6 29.2 %collective-permute-start.9 = (bf16[128,5120]{1,0:T(8,128)(2,1)S(1)}, bf16[128,5120]{1,0:T(8,128)(2,1)S(1)}, u32[]{:S(2)}, u32[]{:S(2)}) collective-permute-start(bf16[128,5120]{1,0:T(8,128)(2,1)S(1)} %collective-permute-done.7), channel_id=1, source_target_pairs={{0,15},{1,0},{2,1},{3,2},{4,3},{5,4},{6,5},{7,6},{8,7},{9,8},{10,9... | collective-permute-start | bytes 3932168 | tf_op jit(solution)/shard_map/ppermute | solution.py:35
  166.4 28.6 %collective-permute-start.10 = (bf16[128,5120]{1,0:T(8,128)(2,1)S(1)}, bf16[128,5120]{1,0:T(8,128)(2,1)S(1)}, u32[]{:S(2)}, u32[]{:S(2)}) collective-permute-start(bf16[128,5120]{1,0:T(8,128)(2,1)S(1)} %collective-permute-done.8), channel_id=1, source_target_pairs={{0,1},{1,2},{2,3},{3,4},{4,5},{5,6},{6,7},{7,8},{8,9},{9,10},{10,1... | collective-permute-start | bytes 3932168 | tf_op jit(solution)/shard_map/ppermute | solution.py:30
  175.8 28.3 %collective-permute-start.11 = (bf16[128,5120]{1,0:T(8,128)(2,1)S(1)}, bf16[128,5120]{1,0:T(8,128)(2,1)S(1)}, u32[]{:S(2)}, u32[]{:S(2)}) collective-permute-start(bf16[128,5120]{1,0:T(8,128)(2,1)S(1)} %collective-permute-done.9), channel_id=1, source_target_pairs={{0,15},{1,0},{2,1},{3,2},{4,3},{5,4},{6,5},{7,6},{8,7},{9,8},{10,9... | collective-permute-start | bytes 3932168 | tf_op jit(solution)/shard_map/ppermute | solution.py:35
  195.0 27.7 %collective-permute-start.12 = (bf16[128,5120]{1,0:T(8,128)(2,1)S(1)}, bf16[128,5120]{1,0:T(8,128)(2,1)S(1)}, u32[]{:S(2)}, u32[]{:S(2)}) collective-permute-start(bf16[128,5120]{1,0:T(8,128)(2,1)S(1)} %collective-permute-done.10), channel_id=1, source_target_pairs={{0,1},{1,2},{2,3},{3,4},{4,5},{5,6},{6,7},{7,8},{8,9},{9,10},{10,1... | collective-permute-start | bytes 3932168 | tf_op jit(solution)/shard_map/ppermute | solution.py:30
  204.1 27.4 %collective-permute-start.13 = (bf16[128,5120]{1,0:T(8,128)(2,1)S(1)}, bf16[128,5120]{1,0:T(8,128)(2,1)S(1)}, u32[]{:S(2)}, u32[]{:S(2)}) collective-permute-start(bf16[128,5120]{1,0:T(8,128)(2,1)S(1)} %collective-permute-done.11), channel_id=1, source_target_pairs={{0,15},{1,0},{2,1},{3,2},{4,3},{5,4},{6,5},{7,6},{8,7},{9,8},{10,9... | collective-permute-start | bytes 3932168 | tf_op jit(solution)/shard_map/ppermute | solution.py:35
  222.7 27.2 %collective-permute-start.14 = (bf16[128,5120]{1,0:T(8,128)(2,1)S(1)}, bf16[128,5120]{1,0:T(8,128)(2,1)S(1)}, u32[]{:S(2)}, u32[]{:S(2)}) collective-permute-start(bf16[128,5120]{1,0:T(8,128)(2,1)S(1)} %collective-permute-done.12), channel_id=1, source_target_pairs={{0,1},{1,2},{2,3},{3,4},{4,5},{5,6},{6,7},{7,8},{8,9},{9,10},{10,1... | collective-permute-start | bytes 3932168 | tf_op jit(solution)/shard_map/ppermute | solution.py:30
  251.1 15.5 %copy-start.5 = (f32[8]{0:T(128)S(1)}, f32[8]{0:T(128)}, u32[]{:S(2)}) copy-start(f32[8]{0:T(128)} %param.15) | copy-start | bytes 100
  251.1 61.1 %copy-start.1 = (f32[640,320]{0,1:T(8,128)S(1)}, f32[640,320]{0,1:T(8,128)}, u32[]{:S(2)}) copy-start(f32[640,320]{0,1:T(8,128)} %param.10) | copy-start | bytes 2457604
  265.1 145.4 %all-gather.2.cloned.1.call-start = ((), (), s32[]{:S(2)}) async-start(), calls=%async_computation.2 | async-start | bytes 3686400 | tf_op jit(solution)/shard_map/all_gather | solution.py:63
Sparse Core Ops, SparseCore 0:
  265.2 46.9 reduce-scatter.1
  385.0 25.4 all-gather.1
